TPU v7x, 32 devices: a whole 2x2x4 slice. The times are simulated.
32 devices in a mesh: blk: 8 (over z, x), mp: 4 (over y, core).
Axes of the slice: x: 2, y: 2, z: 4, core: 2. Of those that a mesh axis runs over, the one named last changes fastest.
Arguments:
- lengths: int32 [4], replicated, may hold values from 1 to 512, 1024 in all
- groups: int32 [4], replicated, may hold values from 0 to 3, as said below
- deal: int32 [1024], P('blk'), may hold values from 0 to 1023, as said below
- prefix_block: int32 [8], P('blk'), may hold values from 0 to 7, each once
- queries: bfloat16 [1024, 2048], P('blk', 'mp'), may hold values from -8 to 8
- keys: bfloat16 [1024, 512], P('blk', 'mp'), may hold values from -8 to 8
- values: bfloat16 [1024, 512], P('blk', 'mp'), may hold values from -6 to 6
- prefix_key_blocks: bfloat16 [512, 512], P('blk', 'mp'), may hold values from -8 to 8
- prefix_value_blocks: bfloat16 [512, 512], P('blk', 'mp'), may hold values from -6 to 6
- out_weight: bfloat16 [2048, 4096], P('mp'), may hold values from -0.125 to 0.125
Outputs:
- layer_out: bfloat16 [1024, 4096], P('blk', 'mp')
Inputs may be any that keep to these rules, and one draw needn't show every extreme that they name: The 4 lengths sum to 1024; the largest is 512. `groups`: each group has exactly 1 request. `deal`: a permutation of the request-order rows; on every index of blk, the 16 slots c * 16 to c * 16 + 15 hold rows taken from request-order rows c * 128 to c * 128 + 127, and over all indices of blk each of those rows appears once. `prefix_block`: a permutation of the blocks.
All inputs are finite; a program needn't handle non-finite values.
Results may differ from a plain program's by a relative error of at most 0.012.
Values may be sent and summed in bfloat16 or wider, within the bound.
A program may use at most 64 MiB of HBM per device.

v0:
```python
import math
import jax
import jax.numpy as jnp
from jax import lax
from jax.sharding import PartitionSpec as P

HEAD_WIDTH = 128
GROUPS = 4
NEGATIVE = -1e30


def request_index(row_ids, req_ends):
    return jnp.sum((row_ids[:, None] >= req_ends[None, :]).astype(jnp.int32), axis=1)


def lookup(values_table, indices):
    slots = jnp.arange(values_table.shape[0], dtype=jnp.int32)
    return jnp.sum(jnp.where(indices[:, None] == slots[None, :], values_table[None, :], 0), axis=1)


def attend(flash_state, grouped, key_block, value_block, visible):
    run_best, run_total, run_accum = flash_state
    key_count = key_block.shape[0]
    kv_heads = grouped.shape[1]
    head_size = grouped.shape[3]
    score_scale = 1.0 / math.sqrt(head_size)
    keys_three = key_block.reshape(key_count, kv_heads, head_size)
    values_three = value_block.reshape(key_count, kv_heads, head_size)
    scores = (
        jnp.einsum("rgjd,ngd->rgjn", grouped, keys_three, preferred_element_type=jnp.float32)
        * score_scale
    )
    shown = visible[:, None, None, :]
    scores = jnp.where(shown, scores, NEGATIVE)
    new_best = jnp.maximum(run_best, jnp.max(scores, axis=3))
    weights = jnp.where(shown, jnp.exp(scores - new_best[..., None]), 0.0)
    factor = jnp.exp(run_best - new_best)
    run_total = run_total * factor + jnp.sum(weights, axis=3)
    mixed = jnp.einsum(
        "rgjn,ngd->rgjd",
        weights.astype(jnp.bfloat16),
        values_three,
        preferred_element_type=jnp.float32,
    )
    run_accum = run_accum * factor[..., None] + mixed
    return (new_best, run_total, run_accum)


def sweep(flash_state, grouped, key_block, value_block, key_info, visible_of):
    key_count = key_block.shape[0]
    step_width = key_count if key_count <= 1024 else math.gcd(key_count, 512)
    if step_width == key_count:
        return attend(flash_state, grouped, key_block, value_block, visible_of(key_info))

    def one_step(carried, step_index):
        offset = step_index * step_width
        key_part = lax.dynamic_slice_in_dim(key_block, offset, step_width, 0)
        value_part = lax.dynamic_slice_in_dim(value_block, offset, step_width, 0)
        info_part = lax.dynamic_slice_in_dim(key_info, offset, step_width, 0)
        return (attend(carried, grouped, key_part, value_part, visible_of(info_part)), None)

    flash_state, _ = lax.scan(
        one_step, flash_state, jnp.arange(key_count // step_width, dtype=jnp.int32)
    )
    return flash_state


def shards(
    lengths,
    groups,
    deal,
    prefix_block,
    queries,
    keys,
    values,
    prefix_key_blocks,
    prefix_value_blocks,
    out_weight,
):
    count_rows = queries.shape[0]
    kv_heads = keys.shape[1] // HEAD_WIDTH
    query_per_key_head = queries.shape[1] // keys.shape[1]
    devices = lax.axis_size("blk")
    my_index = lax.axis_index("blk")
    piece_rows = count_rows // devices
    per_group = devices // GROUPS
    prefix_rows = prefix_key_blocks.shape[0]
    req_ends = jnp.cumsum(lengths)
    arrived = lax.all_to_all(
        deal.reshape(devices, piece_rows), "blk", split_axis=0, concat_axis=0, tiled=True
    )
    placed = arrived.reshape(count_rows) - my_index * count_rows

    def prefix_pass(flash_state, grouped, query_group, block_ids):

        def prefix_step(carried, kv_piece):
            key_count = kv_piece[0].shape[0]
            owners = jnp.arange(key_count, dtype=jnp.int32) // prefix_rows
            key_group = jnp.take(block_ids, owners) // per_group

            def same_group(key_info):
                return key_info[None, :] == query_group[:, None]

            return sweep(carried, grouped, kv_piece[0], kv_piece[1], key_group, same_group)

        return prefix_step(
            flash_state,
            (
                lax.all_gather(prefix_key_blocks, "blk", axis=0, tiled=True),
                lax.all_gather(prefix_value_blocks, "blk", axis=0, tiled=True),
            ),
        )

    def suffix_rule(query_rows, query_req):

        def same_request(key_info):
            key_req = request_index(key_info, req_ends)
            return (
                (key_info[None, :] >= 0)
                & (key_req[None, :] == query_req[:, None])
                & (key_info[None, :] <= query_rows[:, None])
            )

        return same_request

    key_rows, block_ids = (
        lax.all_gather(deal, "blk", axis=0, tiled=True),
        lax.all_gather(prefix_block, "blk", axis=0, tiled=True),
    )
    query_rows = deal
    query_req = request_index(query_rows, req_ends)
    query_group = lookup(groups, query_req)
    grouped = queries.reshape(count_rows, kv_heads, query_per_key_head, HEAD_WIDTH)
    flash_state = prefix_pass(
        (
            jnp.full((count_rows, kv_heads, query_per_key_head), NEGATIVE, jnp.float32),
            jnp.zeros((count_rows, kv_heads, query_per_key_head), jnp.float32),
            jnp.zeros((count_rows, kv_heads, query_per_key_head, HEAD_WIDTH), jnp.float32),
        ),
        grouped,
        query_group,
        block_ids,
    )
    visible_of = suffix_rule(query_rows, query_req)
    kv_piece = (
        lax.all_gather(keys, "blk", axis=0, tiled=True),
        lax.all_gather(values, "blk", axis=0, tiled=True),
    )
    key_info = key_rows
    flash_state = sweep(flash_state, grouped, kv_piece[0], kv_piece[1], key_info, visible_of)
    run_best, run_total, run_accum = flash_state
    attended = (run_accum / run_total[..., None]).astype(jnp.bfloat16).reshape(count_rows, -1)
    returned = lax.all_to_all(
        attended.reshape(devices, piece_rows, -1), "blk", split_axis=0, concat_axis=0, tiled=True
    )
    flat = returned.reshape(count_rows, returned.shape[2])
    ordered = jnp.zeros_like(flat).at[placed].set(flat)
    partial_value = jnp.dot(ordered, out_weight, preferred_element_type=jnp.float32)
    return lax.psum_scatter(
        partial_value.astype(jnp.bfloat16), "mp", scatter_dimension=1, tiled=True
    )


def solution(mesh):
    return jax.shard_map(
        shards,
        mesh=mesh,
        in_specs=(
            P(),
            P(),
            P("blk"),
            P("blk"),
            P("blk", "mp"),
            P("blk", "mp"),
            P("blk", "mp"),
            P("blk", "mp"),
            P("blk", "mp"),
            P("mp", None),
        ),
        out_specs=P("blk", "mp"),
        check_vma=False,
    )
```

profile of v0, /device:TPU:0, one launch (start us, length us, event | category | flops | bytes accessed | tf_op | source)
XLA Modules:
  0.0 230.1 jit_solution(1636237273558272072)
XLA Ops:
  6.5 1.4 all_to_all.9
  7.9 7.3 %all-to-all-start = ((s32[8,1,16]{2,1,0:T(1,128)}), s32[8,1,16]{2,1,0:T(1,128)S(1)}, u32[]{:S(2)}, u32[]{:S(2)}) async-start(s32[8,1,16]{2,1,0:T(1,128)} %bitcast), calls=%async_computation | async-start | bytes 8192 | tf_op jit(solution)/shard_map/all_to_all | solution.py:89
  15.2 0.8 reduce-window.8
  16.0 0.7 convert_reduce_fusion.1
  16.7 21.0 %all-gather = s32[8,1,128]{2,1,0:T(1,128)S(1)} all-gather(s32[1,1,128]{2,1,0:T(1,128)} %bitcast.108), channel_id=1, replica_groups=mesh['blk'=8,'mp'=4] {'blk'}, dimensions={0}, use_global_device_ids=true | all-gather | bytes 4608 | tf_op jit(solution)/shard_map/all_gather | solution.py:127
  38.5 1.2 dynamic-slice
  39.7 0.8 dynamic-update-slice
  40.5 6.8 %all-reduce = s32[8]{0:T(128)S(1)} all-reduce(s32[8]{0:T(128)S(1)} %dynamic-update-slice), channel_id=1, replica_groups=mesh['blk'=8,'mp'=4] {'blk'}, use_global_device_ids=true, to_apply=%add | all-reduce | flops 8 | bytes 64
  47.3 0.7 fusion.47
  48.0 32.5 %all_gather.19 = bf16[512,128]{1,0:T(8,128)(2,1)S(1)} all-gather(bf16[64,128]{1,0:T(8,128)(2,1)} %param.17), channel_id=1, replica_groups=mesh['blk'=8,'mp'=4] {'blk'}, dimensions={0}, use_global_device_ids=true | all-gather | bytes 147456 | tf_op jit(solution)/shard_map/all_gather | solution.py:109
  80.5 30.9 %all_gather.22 = bf16[1024,128]{1,0:T(8,128)(2,1)S(1)} all-gather(bf16[128,128]{1,0:T(8,128)(2,1)} %param.15), channel_id=1, replica_groups=mesh['blk'=8,'mp'=4] {'blk'}, dimensions={0}, use_global_device_ids=true | all-gather | bytes 294912 | tf_op jit(solution)/shard_map/all_gather | solution.py:146
  111.5 31.0 %all_gather.23 = bf16[1024,128]{1,0:T(8,128)(2,1)S(1)} all-gather(bf16[128,128]{1,0:T(8,128)(2,1)} %param.16), channel_id=1, replica_groups=mesh['blk'=8,'mp'=4] {'blk'}, dimensions={0}, use_global_device_ids=true | all-gather | bytes 294912 | tf_op jit(solution)/shard_map/all_gather | solution.py:147
  142.5 0.7 select_reduce_fusion
  143.2 4.3 %compare_select_fusion.1 = s32[512,1]{0,1:T(1,128)S(1)} fusion(s32[]{:T(128)} %bitcast.4, s32[]{:T(128)} %bitcast.5, s32[]{:T(128)} %bitcast.6, s32[]{:T(128)} %bitcast.7, s32[]{:T(128)} %bitcast.8, s32[]{:T(128)} %bitcast.10, s32[]{:T(128)} %bitcast.9), kind=kLoop, calls=%fused_computation.47 | loop fusion | flops 11776 | bytes 2076 | tf_op jit(solution)/shard_map/jit(_take)/gather | solution.py:99
  147.6 0.7 add_select_fusion
  148.4 1.5 compare_and_fusion
  151.3 0.8 convolution_bitcast_fusion.1
  152.0 30.5 %all_gather.20 = bf16[512,128]{1,0:T(8,128)(2,1)S(1)} all-gather(bf16[64,128]{1,0:T(8,128)(2,1)S(1)} %copy-done.1), channel_id=1, replica_groups=mesh['blk'=8,'mp'=4] {'blk'}, dimensions={0}, use_global_device_ids=true | all-gather | bytes 147456 | tf_op jit(solution)/shard_map/all_gather | solution.py:110
  183.4 0.7 reshape_reshape.3
  184.1 4.0 %all-to-all-start.1 = ((bf16[8,16,512]{2,1,0:T(8,128)(2,1)}), bf16[8,16,512]{2,1,0:T(8,128)(2,1)S(1)}, u32[]{:S(2)}, u32[]{:S(2)}) async-start(bf16[8,16,512]{2,1,0:T(8,128)(2,1)} %reshape_reshape.3), calls=%async_computation.1 | async-start | bytes 262144 | tf_op jit(solution)/shard_map/all_to_all | solution.py:153
  188.2 7.2 %all-to-all-done.1 = bf16[8,16,512]{2,1,0:T(8,128)(2,1)S(1)} async-done(((bf16[8,16,512]{2,1,0:T(8,128)(2,1)}), bf16[8,16,512]{2,1,0:T(8,128)(2,1)S(1)}, u32[]{:S(2)}, u32[]{:S(2)}) %all-to-all-start.1) | async-done | bytes 131104 | tf_op jit(solution)/shard_map/all_to_all | solution.py:153
  195.4 1.1 scatter_custom_fusion
  196.5 3.9 %convolution_convert_fusion = bf16[128,4096]{1,0:T(8,128)(2,1)} fusion(bf16[128,512]{1,0:T(8,128)(2,1)S(1)} %scatter_custom_fusion, bf16[512,4096]{1,0:T(8,128)(2,1)} %param.19), kind=kOutput, calls=%fused_computation.1 | convolution fusion | flops 537395200 | bytes 5373952 | tf_op jit(solution)/shard_map/dot_general | solution.py:158
  200.4 22.9 %reduce-scatter.2.cloned.1.call-done = bf16[128,1024]{1,0:T(8,128)(2,1)} async-done(((bf16[128,4096]{1,0:T(8,128)(2,1)}), bf16[128,1024]{1,0:T(8,128)(2,1)}) %reduce-scatter.2.cloned.1.call-update) | async-done | bytes 262160 | tf_op jit(solution)/shard_map/reduce_scatter | solution.py:159
  (23 shorter events, 2.5 us)
Async XLA Ops:
  6.5 143.4 %copy-start = (bf16[128,512]{1,0:T(8,128)(2,1)S(1)}, bf16[128,512]{1,0:T(8,128)(2,1)}, u32[]{:S(2)}) copy-start(bf16[128,512]{1,0:T(8,128)(2,1)} %param.14) | copy-start | bytes 393220
  7.9 176.2 %all-to-all-start = ((s32[8,1,16]{2,1,0:T(1,128)}), s32[8,1,16]{2,1,0:T(1,128)S(1)}, u32[]{:S(2)}, u32[]{:S(2)}) async-start(s32[8,1,16]{2,1,0:T(1,128)} %bitcast), calls=%async_computation | async-start | bytes 8192 | tf_op jit(solution)/shard_map/all_to_all | solution.py:89
  151.2 0.8 copy-start.1
  184.1 11.3 %all-to-all-start.1 = ((bf16[8,16,512]{2,1,0:T(8,128)(2,1)}), bf16[8,16,512]{2,1,0:T(8,128)(2,1)S(1)}, u32[]{:S(2)}, u32[]{:S(2)}) async-start(bf16[8,16,512]{2,1,0:T(8,128)(2,1)} %reshape_reshape.3), calls=%async_computation.1 | async-start | bytes 262144 | tf_op jit(solution)/shard_map/all_to_all | solution.py:153
  188.1 35.2 %reduce-scatter.2.cloned.1.call-start = ((), (), s32[]{:S(2)}) async-start(), calls=%async_computation.3 | async-start | bytes 1310720 | tf_op jit(solution)/shard_map/reduce_scatter | solution.py:159
Sparse Core Ops, SparseCore 0:
  200.5 22.6 reduce-scatter.1
where the time goes:
time: 231 us; the launch traced here: 230 us
  blocking collectives  153 us (66%)
  waiting for transfers between devices  30.1 us (13%)
  between operations  14.2 us (6%)
  starting transfers between devices  11.3 us (5%)
  other arithmetic  9.85 us (4%)
  local copies, waits for them, and re-layouts  6.03 us (3%)
  matrix products  5.89 us (3%)
    all_gather x1, blocking collectives, prefix_pass(): lax.all_gather(prefix_key_blocks, 'blk', axis=0, tiled=True)  32.5 us
    all_gather x1, blocking collectives, shards(): lax.all_gather(values, 'blk', axis=0, tiled=True)  31 us
    all_gather x1, blocking collectives, shards(): lax.all_gather(keys, 'blk', axis=0, tiled=True)  30.9 us
    all_gather x1, blocking collectives, prefix_pass(): lax.all_gather(prefix_value_blocks, 'blk', axis=0, tiled=True)  30.5 us
    reduce_scatter x1, waiting for transfers between devices, shards(): lax.psum_scatter(partial_value.astype(jnp.bfloat16), 'mp', scatter_dimens...  22.9 us
    all_gather x1, blocking collectives, shards(): lax.all_gather(deal, 'blk', axis=0, tiled=True)  21 us
    all_to_all x1, starting transfers between devices, shards(): lax.all_to_all(deal.reshape(devices, piece_rows), 'blk', split_axis=0, co...  7.25 us
    all_to_all x1, waiting for transfers between devices, shards(): lax.all_to_all(attended.reshape(devices, piece_rows, -1), 'blk', split_ax...  7.19 us
  transfers between devices with their start and end apart: 3, of which 2 were waited for; matrix products, arithmetic and copies ran while one was open for 7% of the time, Pallas kernels for 0%

commit v1 on v0

--- a/solution.py
+++ b/solution.py
@@ -7,6 +7,27 @@
 HEAD_WIDTH = 128
 GROUPS = 4
 NEGATIVE = -1e30
+
+
+def collect(x, axis, dim):
+    count, position, width = (lax.axis_size(axis), lax.axis_index(axis), x.shape[dim])
+    upward = [(i, (i + 1) % count) for i in range(count)]
+    downward = [(i, (i - 1) % count) for i in range(count)]
+    filled = jnp.zeros((*x.shape[:dim], count * width, *x.shape[dim + 1 :]), x.dtype)
+    filled = lax.dynamic_update_slice_in_dim(filled, x, position * width, axis=dim)
+    from_left = from_right = x
+    half = count // 2
+    for step in range(1, half + 1):
+        from_left = lax.ppermute(from_left, axis, upward)
+        filled = lax.dynamic_update_slice_in_dim(
+            filled, from_left, (position - step) % count * width, axis=dim
+        )
+        if step < count - half:
+            from_right = lax.ppermute(from_right, axis, downward)
+            filled = lax.dynamic_update_slice_in_dim(
+                filled, from_right, (position + step) % count * width, axis=dim
+            )
+    return filled
 
 
 def request_index(row_ids, req_ends):
@@ -106,7 +127,7 @@
         return prefix_step(
             flash_state,
             (
-                lax.all_gather(prefix_key_blocks, "blk", axis=0, tiled=True),
+                collect(prefix_key_blocks, "blk", 0),
                 lax.all_gather(prefix_value_blocks, "blk", axis=0, tiled=True),
             ),
         )

time: 231 us -> 222 us (0.961)
  blocking collectives: 153 us -> 122 us
  starting transfers between devices: 11.3 us -> 22.2 us
  waiting for transfers between devices: 30.1 us -> 39.9 us
    all_gather x1 -> x0, blocking collectives: 32.5 us -> none  [prefix_pass(): lax.all_gather(prefix_key_blocks, 'blk', axis=0, tiled=True)]
    ppermute x0 -> x7, starting transfers between devices: none -> 15.4 us  [the longest x3 12.5 us: collect(): from_right = lax.ppermute(from_right, axis, downward)]
    ppermute x0 -> x7, waiting for transfers between devices: none -> 9.8 us  [the longest x4 9.79 us: collect(): from_left = lax.ppermute(from_left, axis, upward)]
    all_to_all x1, starting transfers between devices: 7.25 us -> 3.33 us  [shards(): lax.all_to_all(deal.reshape(devices, piece_rows), 'blk', split_axis=0, co...]
  transfers between devices with their start and end apart: 3 -> 10, of which waited for: 2 -> 5; matrix products, arithmetic and copies ran while one was open for 7% -> 7% of each run, Pallas kernels for 0% -> 0%
where the time goes in v1:
time: 222 us; the launch traced here: 221 us
  blocking collectives  122 us (55%)
  waiting for transfers between devices  39.9 us (18%)
  starting transfers between devices  22.2 us (10%)
  between operations  14.2 us (6%)
  other arithmetic  9.86 us (4%)
  local copies, waits for them, and re-layouts  6.81 us (3%)
  matrix products  5.88 us (3%)
    all_gather x1, blocking collectives, shards(): lax.all_gather(keys, 'blk', axis=0, tiled=True)  32.7 us
    all_gather x1, blocking collectives, shards(): lax.all_gather(values, 'blk', axis=0, tiled=True)  31 us
    all_gather x1, blocking collectives, prefix_pass(): lax.all_gather(prefix_value_blocks, 'blk', axis=0, tiled=True)  30.8 us
    reduce_scatter x1, waiting for transfers between devices, shards(): lax.psum_scatter(partial_value.astype(jnp.bfloat16), 'mp', scatter_dimens...  22.9 us
    all_gather x1, blocking collectives, shards(): lax.all_gather(deal, 'blk', axis=0, tiled=True)  21 us
    ppermute x3, starting transfers between devices, collect(): from_right = lax.ppermute(from_right, axis, downward)  12.5 us
    ppermute x4, waiting for transfers between devices, collect(): from_left = lax.ppermute(from_left, axis, upward)  9.79 us
    all_to_all x1, waiting for transfers between devices, shards(): lax.all_to_all(attended.reshape(devices, piece_rows, -1), 'blk', split_ax...  7.12 us
  transfers between devices with their start and end apart: 10, of which 5 were waited for; matrix products, arithmetic and copies ran while one was open for 7% of the time, Pallas kernels for 0%

profile of v1, /device:TPU:0, one launch (start us, length us, event | category | flops | bytes accessed | tf_op | source)
XLA Modules:
  0.0 221.1 jit_solution(3949350005986247833)
XLA Ops:
  6.5 2.9 %collective-permute-start = (bf16[64,128]{1,0:T(8,128)(2,1)}, bf16[64,128]{1,0:T(8,128)(2,1)S(1)}, u32[]{:S(2)}, u32[]{:S(2)}) collective-permute-start(bf16[64,128]{1,0:T(8,128)(2,1)} %param.17), channel_id=1, source_target_pairs={{0,4},{4,8},{8,12},{12,16},{16,20},{20,24},{24,28},{28,0},{1,5},{5... | collective-permute-start | bytes 49160 | tf_op jit(solution)/shard_map/ppermute | solution.py:21
  9.5 3.0 %collective-permute-start.1 = (bf16[64,128]{1,0:T(8,128)(2,1)}, bf16[64,128]{1,0:T(8,128)(2,1)S(1)}, u32[]{:S(2)}, u32[]{:S(2)}) collective-permute-start(bf16[64,128]{1,0:T(8,128)(2,1)} %param.17), channel_id=1, source_target_pairs={{0,28},{4,0},{8,4},{12,8},{16,12},{20,16},{24,20},{28,24},{1,29},{... | collective-permute-start | bytes 49160 | tf_op jit(solution)/shard_map/ppermute | solution.py:26
  12.5 1.3 all_to_all.9
  13.8 3.3 %all-to-all-start = ((s32[8,1,16]{2,1,0:T(1,128)}), s32[8,1,16]{2,1,0:T(1,128)S(1)}, u32[]{:S(2)}, u32[]{:S(2)}) async-start(s32[8,1,16]{2,1,0:T(1,128)} %bitcast), calls=%async_computation | async-start | bytes 8192 | tf_op jit(solution)/shard_map/all_to_all | solution.py:110
  17.2 0.8 reduce-window.8
  18.8 21.0 %all-gather = s32[8,1,128]{2,1,0:T(1,128)S(1)} all-gather(s32[1,1,128]{2,1,0:T(1,128)} %bitcast.108), channel_id=1, replica_groups=mesh['blk'=8,'mp'=4] {'blk'}, dimensions={0}, use_global_device_ids=true | all-gather | bytes 4608 | tf_op jit(solution)/shard_map/all_gather | solution.py:148
  40.5 1.2 dynamic-slice
  41.8 0.8 dynamic-update-slice
  42.5 6.8 %all-reduce = s32[8]{0:T(128)S(1)} all-reduce(s32[8]{0:T(128)S(1)} %dynamic-update-slice), channel_id=1, replica_groups=mesh['blk'=8,'mp'=4] {'blk'}, use_global_device_ids=true, to_apply=%add | all-reduce | flops 8 | bytes 64
  50.0 32.7 %all_gather.18 = bf16[1024,128]{1,0:T(8,128)(2,1)S(1)} all-gather(bf16[128,128]{1,0:T(8,128)(2,1)} %param.15), channel_id=1, replica_groups=mesh['blk'=8,'mp'=4] {'blk'}, dimensions={0}, use_global_device_ids=true | all-gather | bytes 294912 | tf_op jit(solution)/shard_map/all_gather | solution.py:167
  82.7 31.0 %all_gather.19 = bf16[1024,128]{1,0:T(8,128)(2,1)S(1)} all-gather(bf16[128,128]{1,0:T(8,128)(2,1)} %param.16), channel_id=1, replica_groups=mesh['blk'=8,'mp'=4] {'blk'}, dimensions={0}, use_global_device_ids=true | all-gather | bytes 294912 | tf_op jit(solution)/shard_map/all_gather | solution.py:168
  115.2 4.3 %compare_select_fusion.1 = s32[512,1]{0,1:T(1,128)S(1)} fusion(s32[]{:T(128)} %bitcast.4, s32[]{:T(128)} %bitcast.5, s32[]{:T(128)} %bitcast.6, s32[]{:T(128)} %bitcast.7, s32[]{:T(128)} %bitcast.8, s32[]{:T(128)} %bitcast.10, s32[]{:T(128)} %bitcast.9), kind=kLoop, calls=%fused_computation.47 | loop fusion | flops 11776 | bytes 2076 | tf_op jit(solution)/shard_map/jit(_take)/gather | solution.py:120
  120.3 1.5 compare_and_fusion
  122.4 30.8 %all_gather.16 = bf16[512,128]{1,0:T(8,128)(2,1)S(1)} all-gather(bf16[64,128]{1,0:T(8,128)(2,1)S(1)} %copy-done.1), channel_id=1, replica_groups=mesh['blk'=8,'mp'=4] {'blk'}, dimensions={0}, use_global_device_ids=true | all-gather | bytes 147456 | tf_op jit(solution)/shard_map/all_gather | solution.py:131
  153.2 4.7 %collective-permute-start.3 = (bf16[64,128]{1,0:T(8,128)(2,1)S(1)}, bf16[64,128]{1,0:T(8,128)(2,1)S(1)}, u32[]{:S(2)}, u32[]{:S(2)}) collective-permute-start(bf16[64,128]{1,0:T(8,128)(2,1)S(1)} %collective-permute-done.1), channel_id=1, source_target_pairs={{0,28},{4,0},{8,4},{12,8},{16,12},{20,16},{24,20},{28,24},{1,29},{... | collective-permute-start | bytes 49160 | tf_op jit(solution)/shard_map/ppermute | solution.py:26
  157.9 1.7 collective-permute-done.2
  159.6 4.7 %collective-permute-start.5 = (bf16[64,128]{1,0:T(8,128)(2,1)S(1)}, bf16[64,128]{1,0:T(8,128)(2,1)S(1)}, u32[]{:S(2)}, u32[]{:S(2)}) collective-permute-start(bf16[64,128]{1,0:T(8,128)(2,1)S(1)} %collective-permute-done.3), channel_id=1, source_target_pairs={{0,28},{4,0},{8,4},{12,8},{16,12},{20,16},{24,20},{28,24},{1,29},{... | collective-permute-start | bytes 49160 | tf_op jit(solution)/shard_map/ppermute | solution.py:26
  164.3 1.7 collective-permute-done.4
  166.1 6.4 %collective-permute-done.6 = bf16[64,128]{1,0:T(8,128)(2,1)S(1)} collective-permute-done((bf16[64,128]{1,0:T(8,128)(2,1)S(1)}, bf16[64,128]{1,0:T(8,128)(2,1)S(1)}, u32[]{:S(2)}, u32[]{:S(2)}) %collective-permute-start.6) | collective-permute-done | bytes 16416 | tf_op jit(solution)/shard_map/ppermute | solution.py:21
  175.6 3.4 %all-to-all-start.1 = ((bf16[8,16,512]{2,1,0:T(8,128)(2,1)}), bf16[8,16,512]{2,1,0:T(8,128)(2,1)S(1)}, u32[]{:S(2)}, u32[]{:S(2)}) async-start(bf16[8,16,512]{2,1,0:T(8,128)(2,1)} %reshape_reshape.3), calls=%async_computation.1 | async-start | bytes 262144 | tf_op jit(solution)/shard_map/all_to_all | solution.py:174
  179.2 7.1 %all-to-all-done.1 = bf16[8,16,512]{2,1,0:T(8,128)(2,1)S(1)} async-done(((bf16[8,16,512]{2,1,0:T(8,128)(2,1)}), bf16[8,16,512]{2,1,0:T(8,128)(2,1)S(1)}, u32[]{:S(2)}, u32[]{:S(2)}) %all-to-all-start.1) | async-done | bytes 131104 | tf_op jit(solution)/shard_map/all_to_all | solution.py:174
  186.3 1.1 scatter_custom_fusion
  187.4 3.9 %convolution_convert_fusion = bf16[128,4096]{1,0:T(8,128)(2,1)} fusion(bf16[128,512]{1,0:T(8,128)(2,1)S(1)} %scatter_custom_fusion, bf16[512,4096]{1,0:T(8,128)(2,1)} %param.19), kind=kOutput, calls=%fused_computation.1 | convolution fusion | flops 537395200 | bytes 5373952 | tf_op jit(solution)/shard_map/dot_general | solution.py:179
  191.3 22.9 %reduce-scatter.2.cloned.1.call-done = bf16[128,1024]{1,0:T(8,128)(2,1)} async-done(((bf16[128,4096]{1,0:T(8,128)(2,1)}), bf16[128,1024]{1,0:T(8,128)(2,1)}) %reduce-scatter.2.cloned.1.call-update) | async-done | bytes 262160 | tf_op jit(solution)/shard_map/reduce_scatter | solution.py:180
  (45 shorter events, 7.7 us)
Async XLA Ops:
  6.5 115.4 %copy-start = (bf16[128,512]{1,0:T(8,128)(2,1)S(1)}, bf16[128,512]{1,0:T(8,128)(2,1)}, u32[]{:S(2)}) copy-start(bf16[128,512]{1,0:T(8,128)(2,1)} %param.14) | copy-start | bytes 393220
  6.5 115.8 %copy-start.1 = (bf16[64,128]{1,0:T(8,128)(2,1)S(1)}, bf16[64,128]{1,0:T(8,128)(2,1)}, u32[]{:S(2)}) copy-start(bf16[64,128]{1,0:T(8,128)(2,1)} %param.18) | copy-start | bytes 49156
  6.5 146.6 %collective-permute-start = (bf16[64,128]{1,0:T(8,128)(2,1)}, bf16[64,128]{1,0:T(8,128)(2,1)S(1)}, u32[]{:S(2)}, u32[]{:S(2)}) collective-permute-start(bf16[64,128]{1,0:T(8,128)(2,1)} %param.17), channel_id=1, source_target_pairs={{0,4},{4,8},{8,12},{12,16},{16,20},{20,24},{24,28},{28,0},{1,5},{5... | collective-permute-start | bytes 49160 | tf_op jit(solution)/shard_map/ppermute | solution.py:21
  9.5 143.7 %collective-permute-start.1 = (bf16[64,128]{1,0:T(8,128)(2,1)}, bf16[64,128]{1,0:T(8,128)(2,1)S(1)}, u32[]{:S(2)}, u32[]{:S(2)}) collective-permute-start(bf16[64,128]{1,0:T(8,128)(2,1)} %param.17), channel_id=1, source_target_pairs={{0,28},{4,0},{8,4},{12,8},{16,12},{20,16},{24,20},{28,24},{1,29},{... | collective-permute-start | bytes 49160 | tf_op jit(solution)/shard_map/ppermute | solution.py:26
  13.8 161.8 %all-to-all-start = ((s32[8,1,16]{2,1,0:T(1,128)}), s32[8,1,16]{2,1,0:T(1,128)S(1)}, u32[]{:S(2)}, u32[]{:S(2)}) async-start(s32[8,1,16]{2,1,0:T(1,128)} %bitcast), calls=%async_computation | async-start | bytes 8192 | tf_op jit(solution)/shard_map/all_to_all | solution.py:110
  153.1 6.5 %collective-permute-start.2 = (bf16[64,128]{1,0:T(8,128)(2,1)S(1)}, bf16[64,128]{1,0:T(8,128)(2,1)S(1)}, u32[]{:S(2)}, u32[]{:S(2)}) collective-permute-start(bf16[64,128]{1,0:T(8,128)(2,1)S(1)} %collective-permute-done), channel_id=1, source_target_pairs={{0,4},{4,8},{8,12},{12,16},{16,20},{20,24},{24,28},{28,0},{1,5},{5... | collective-permute-start | bytes 49160 | tf_op jit(solution)/shard_map/ppermute | solution.py:21
  153.2 6.4 %collective-permute-start.3 = (bf16[64,128]{1,0:T(8,128)(2,1)S(1)}, bf16[64,128]{1,0:T(8,128)(2,1)S(1)}, u32[]{:S(2)}, u32[]{:S(2)}) collective-permute-start(bf16[64,128]{1,0:T(8,128)(2,1)S(1)} %collective-permute-done.1), channel_id=1, source_target_pairs={{0,28},{4,0},{8,4},{12,8},{16,12},{20,16},{24,20},{28,24},{1,29},{... | collective-permute-start | bytes 49160 | tf_op jit(solution)/shard_map/ppermute | solution.py:26
  159.6 6.4 %collective-permute-start.4 = (bf16[64,128]{1,0:T(8,128)(2,1)S(1)}, bf16[64,128]{1,0:T(8,128)(2,1)S(1)}, u32[]{:S(2)}, u32[]{:S(2)}) collective-permute-start(bf16[64,128]{1,0:T(8,128)(2,1)S(1)} %collective-permute-done.2), channel_id=1, source_target_pairs={{0,4},{4,8},{8,12},{12,16},{16,20},{20,24},{24,28},{28,0},{1,5},{5... | collective-permute-start | bytes 49160 | tf_op jit(solution)/shard_map/ppermute | solution.py:21
  159.6 6.4 %collective-permute-start.5 = (bf16[64,128]{1,0:T(8,128)(2,1)S(1)}, bf16[64,128]{1,0:T(8,128)(2,1)S(1)}, u32[]{:S(2)}, u32[]{:S(2)}) collective-permute-start(bf16[64,128]{1,0:T(8,128)(2,1)S(1)} %collective-permute-done.3), channel_id=1, source_target_pairs={{0,28},{4,0},{8,4},{12,8},{16,12},{20,16},{24,20},{28,24},{1,29},{... | collective-permute-start | bytes 49160 | tf_op jit(solution)/shard_map/ppermute | solution.py:26
  166.0 6.4 %collective-permute-start.6 = (bf16[64,128]{1,0:T(8,128)(2,1)S(1)}, bf16[64,128]{1,0:T(8,128)(2,1)S(1)}, u32[]{:S(2)}, u32[]{:S(2)}) collective-permute-start(bf16[64,128]{1,0:T(8,128)(2,1)S(1)} %collective-permute-done.4), channel_id=1, source_target_pairs={{0,4},{4,8},{8,12},{12,16},{16,20},{20,24},{24,28},{28,0},{1,5},{5... | collective-permute-start | bytes 49160 | tf_op jit(solution)/shard_map/ppermute | solution.py:21
  175.6 10.7 %all-to-all-start.1 = ((bf16[8,16,512]{2,1,0:T(8,128)(2,1)}), bf16[8,16,512]{2,1,0:T(8,128)(2,1)S(1)}, u32[]{:S(2)}, u32[]{:S(2)}) async-start(bf16[8,16,512]{2,1,0:T(8,128)(2,1)} %reshape_reshape.3), calls=%async_computation.1 | async-start | bytes 262144 | tf_op jit(solution)/shard_map/all_to_all | solution.py:174
  179.0 35.2 %reduce-scatter.2.cloned.1.call-start = ((), (), s32[]{:S(2)}) async-start(), calls=%async_computation.3 | async-start | bytes 1310720 | tf_op jit(solution)/shard_map/reduce_scatter | solution.py:180
Sparse Core Ops, SparseCore 0:
  191.4 22.7 reduce-scatter.1
